TPU v7x, 128 devices: a whole 4x4x4 slice. The times are simulated.
128 devices in a mesh: dp: 64 (over y, x_lo, z, core), tensor: 2 (over x_hi).
Axes of the slice: x: 4 (x_hi: 2, x_lo: 2; x = x_hi * 2 + x_lo), y: 4, z: 4, core: 2. Of those that a mesh axis runs over, the one named last changes fastest.
Arguments:
- tokens: bfloat16 [64, 512, 896], P(None, 'dp'), may hold values from -6 to 6
- cotangent: bfloat16 [64, 512, 896], P(None, 'dp'), may hold values from -6 to 6
- lengths: int32 [64], replicated, may hold values from 1 to 512, 24576 in all
- deal_order: int32 [64], replicated, may hold values from 0 to 63, each once
- gain_attn: bfloat16 [896], replicated, may hold values from 0.099609375 to 1.8984375
- w_query: bfloat16 [896, 896], P(None, 'tensor'), may hold values from -0.1875 to 0.1875
- b_query: bfloat16 [896], P('tensor'), may hold values from -3 to 3
- w_key: bfloat16 [896, 128], P(None, 'tensor'), may hold values from -0.1875 to 0.1875
- b_key: bfloat16 [128], P('tensor'), may hold values from -3 to 3
- w_value: bfloat16 [896, 128], P(None, 'tensor'), may hold values from -0.1875 to 0.1875
- b_value: bfloat16 [128], P('tensor'), may hold values from -3 to 3
- w_out: bfloat16 [896, 896], P('tensor'), may hold values from -1 to 1
- gain_mlp: bfloat16 [896], replicated, may hold values from 0.099609375 to 1.8984375
- w_gate: bfloat16 [896, 4864], P(None, 'tensor'), may hold values from -0.1875 to 0.1875
- w_up: bfloat16 [896, 4864], P(None, 'tensor'), may hold values from -0.1875 to 0.1875
- w_down: bfloat16 [4864, 896], P('tensor'), may hold values from -0.078125 to 0.078125
Outputs:
- layer_out: bfloat16 [64, 512, 896], P(None, 'dp')
- grad_tokens: bfloat16 [64, 512, 896], P(None, 'dp')
- grad_gain_attn: float32 [896], replicated
- grad_w_query: float32 [896, 896], P(None, 'tensor')
- grad_b_query: float32 [896], P('tensor')
- grad_w_key: float32 [896, 128], P(None, 'tensor')
- grad_b_key: float32 [128], P('tensor')
- grad_w_value: float32 [896, 128], P(None, 'tensor')
- grad_b_value: float32 [128], P('tensor')
- grad_w_out: float32 [896, 896], P('tensor')
- grad_gain_mlp: float32 [896], replicated
- grad_w_gate: float32 [896, 4864], P(None, 'tensor')
- grad_w_up: float32 [896, 4864], P(None, 'tensor')
- grad_w_down: float32 [4864, 896], P('tensor')
- rms_values: float32 [3], replicated
Inputs may be any that keep to these rules, and one draw needn't show every extreme that they name: Group g receives stored slot deal_order[g]; every slot goes to exactly one group. The first lengths[g] rows of the slot that group g receives are valid.
All inputs are finite; a program needn't handle non-finite values.
Results may differ from a plain program's by a relative error of at most 0.022.
Values may be sent and summed in bfloat16 or wider, within the bound.
A program may use at most 192 MiB of HBM per device.

v0:
```python
import math
import jax
import jax.numpy as jnp
from jax import lax
from jax.sharding import PartitionSpec as P

HD = 64
epsilon = 1e-06
rope_base = 1000000.0


def rope_tables(seq_rows, head_size):
    places = jnp.arange(seq_rows).astype(jnp.float32)
    frequency = rope_base ** (-jnp.arange(head_size // 2).astype(jnp.float32) * 2.0 / head_size)
    angles = places[:, None] * frequency[None, :]
    return (jnp.cos(angles)[:, None, :], jnp.sin(angles)[:, None, :])


def rotate(tensor, cos_table, sine_table):
    half_width = tensor.shape[-1] // 2
    first_half = tensor[..., :half_width]
    second_half = tensor[..., half_width:]
    return jnp.concatenate(
        [
            first_half * cos_table - second_half * sine_table,
            second_half * cos_table + first_half * sine_table,
        ],
        axis=-1,
    )


def unrotate(grad_rot, cos_table, sine_table):
    half_width = grad_rot.shape[-1] // 2
    first_half = grad_rot[..., :half_width]
    second_half = grad_rot[..., half_width:]
    return jnp.concatenate(
        [
            first_half * cos_table + second_half * sine_table,
            second_half * cos_table - first_half * sine_table,
        ],
        axis=-1,
    )


def dot_left(matrix, other):
    return lax.dot_general(
        matrix, other, (((0,), (0,)), ((), ())), preferred_element_type=jnp.float32
    )


def dot_right(matrix, other):
    return lax.dot_general(
        matrix, other, (((1,), (1,)), ((), ())), preferred_element_type=jnp.float32
    )


def on_device(
    tokens,
    cotangent,
    lengths,
    deal_order,
    gain_attn,
    w_query,
    b_query,
    w_key,
    b_key,
    w_value,
    b_value,
    w_out,
    gain_mlp,
    w_gate,
    w_up,
    w_down,
):
    restore = jnp.argsort(deal_order)
    arrived = (
        lax.all_to_all(tokens[deal_order], "dp", split_axis=0, concat_axis=1, tiled=True),
        lax.all_to_all(cotangent[deal_order], "dp", split_axis=0, concat_axis=1, tiled=True),
    )
    stream = arrived[0][0].astype(jnp.float32)
    grad_out = arrived[1][0].astype(jnp.float32)
    seq_rows, width = stream.shape
    head_size = HD
    length = lengths[lax.axis_index("dp")]
    places = jnp.arange(seq_rows)
    usable = places < length
    row_mask = usable[:, None]
    cos_table, sine_table = rope_tables(seq_rows, head_size)
    local_heads = w_query.shape[1] // head_size
    local_kv = w_key.shape[1] // head_size
    group_size = local_heads // local_kv
    score_scale = 1.0 / math.sqrt(head_size)
    allowed = (places[None, :] <= places[:, None]) & usable[None, :]
    gain_one = gain_attn.astype(jnp.float32)
    gain_two = gain_mlp.astype(jnp.float32)
    inverse_one = lax.rsqrt(jnp.mean(stream * stream, axis=-1, keepdims=True) + epsilon)
    normed = (stream * inverse_one * gain_one).astype(jnp.bfloat16)
    q_lin = jnp.dot(normed, w_query, preferred_element_type=jnp.float32) + b_query.astype(
        jnp.float32
    )
    k_lin = jnp.dot(normed, w_key, preferred_element_type=jnp.float32) + b_key.astype(jnp.float32)
    v_lin = jnp.dot(normed, w_value, preferred_element_type=jnp.float32) + b_value.astype(
        jnp.float32
    )
    queries = rotate(q_lin.reshape(seq_rows, local_heads, head_size), cos_table, sine_table).astype(
        jnp.bfloat16
    )
    queries = queries.reshape(seq_rows, local_kv, group_size, head_size)
    keys_rot = rotate(k_lin.reshape(seq_rows, local_kv, head_size), cos_table, sine_table).astype(
        jnp.bfloat16
    )
    values = v_lin.reshape(seq_rows, local_kv, head_size).astype(jnp.bfloat16)
    raw_scores = jnp.einsum("qkgd,pkd->kgqp", queries, keys_rot, preferred_element_type=jnp.float32)
    scores = jnp.where(allowed, raw_scores * score_scale, -1e30)
    top_score = jnp.max(scores, axis=-1, keepdims=True)
    expo = jnp.exp(scores - top_score)
    total = jnp.sum(expo, axis=-1, keepdims=True)
    log_total = top_score + jnp.log(total)
    probs_low = (expo / total).astype(jnp.bfloat16)
    mixed = jnp.einsum("kgqp,pkd->qkgd", probs_low, values, preferred_element_type=jnp.float32)
    mixed = mixed.reshape(seq_rows, local_heads * head_size).astype(jnp.bfloat16)
    attention = lax.psum(jnp.dot(mixed, w_out, preferred_element_type=jnp.float32), "tensor")
    residual = stream + attention
    inverse_two = lax.rsqrt(jnp.mean(residual * residual, axis=-1, keepdims=True) + epsilon)
    normed_two = (residual * inverse_two * gain_two).astype(jnp.bfloat16)
    gate_lin = jnp.dot(normed_two, w_gate, preferred_element_type=jnp.float32)
    up_lin = jnp.dot(normed_two, w_up, preferred_element_type=jnp.float32)
    sigmoid_gate = jax.nn.sigmoid(gate_lin)
    silu_gate = gate_lin * sigmoid_gate
    hidden = (silu_gate * up_lin).astype(jnp.bfloat16)
    mlp_branch = lax.psum(
        jnp.dot(hidden, w_down, preferred_element_type=jnp.float32).astype(jnp.bfloat16), "tensor"
    ).astype(jnp.float32)
    result = jnp.where(row_mask, residual + mlp_branch, 0.0)
    statistics = jnp.stack(
        [
            jnp.sum(result * result),
            jnp.sum(jnp.where(row_mask, attention * attention, 0.0)),
            jnp.sum(jnp.where(row_mask, mlp_branch * mlp_branch, 0.0)),
        ]
    )
    grad_y = jnp.where(row_mask, grad_out, 0.0)
    grad_low = grad_y.astype(jnp.bfloat16)
    grad_w_down = dot_left(hidden, grad_low)
    grad_hidden = dot_right(grad_low, w_down)
    grad_gate = (
        grad_hidden * up_lin * sigmoid_gate * (1.0 + gate_lin * (1.0 - sigmoid_gate))
    ).astype(jnp.bfloat16)
    grad_up = (grad_hidden * silu_gate).astype(jnp.bfloat16)
    grad_w_gate = dot_left(normed_two, grad_gate)
    grad_w_up = dot_left(normed_two, grad_up)
    grad_normed_two = lax.psum(dot_right(grad_gate, w_gate) + dot_right(grad_up, w_up), "tensor")
    grad_gain_mlp = jnp.sum(grad_normed_two * residual * inverse_two, axis=0)
    scaled_two = grad_normed_two * gain_two
    grad_resid = (
        grad_y
        + inverse_two * scaled_two
        - residual * inverse_two**3 * jnp.mean(scaled_two * residual, axis=-1, keepdims=True)
    )
    grad_attn = grad_resid.astype(jnp.bfloat16)
    grad_w_out = dot_left(mixed, grad_attn)
    grad_mixed = dot_right(grad_attn, w_out).astype(jnp.bfloat16)
    grad_mixed = grad_mixed.reshape(seq_rows, local_kv, group_size, head_size)
    probs = jnp.exp(scores - log_total)
    grad_probs = jnp.einsum(
        "qkgd,pkd->kgqp", grad_mixed, values, preferred_element_type=jnp.float32
    )
    grad_values = jnp.einsum(
        "kgqp,qkgd->pkd", probs_low, grad_mixed, preferred_element_type=jnp.float32
    )
    row_inner = jnp.sum(probs * grad_probs, axis=-1, keepdims=True)
    grad_scores = (probs * (grad_probs - row_inner) * score_scale).astype(jnp.bfloat16)
    grad_queries = jnp.einsum(
        "kgqp,pkd->qkgd", grad_scores, keys_rot, preferred_element_type=jnp.float32
    )
    grad_keys = jnp.einsum(
        "kgqp,qkgd->pkd", grad_scores, queries, preferred_element_type=jnp.float32
    )
    grad_q_lin = unrotate(
        grad_queries.reshape(seq_rows, local_heads, head_size), cos_table, sine_table
    )
    grad_q_lin = grad_q_lin.reshape(seq_rows, local_heads * head_size).astype(jnp.bfloat16)
    grad_k_lin = (
        unrotate(grad_keys, cos_table, sine_table)
        .reshape(seq_rows, local_kv * head_size)
        .astype(jnp.bfloat16)
    )
    grad_v_lin = grad_values.reshape(seq_rows, local_kv * head_size).astype(jnp.bfloat16)
    grad_w_query = dot_left(normed, grad_q_lin)
    grad_w_key = dot_left(normed, grad_k_lin)
    grad_w_value = dot_left(normed, grad_v_lin)
    grad_b_query = jnp.sum(grad_q_lin.astype(jnp.float32), axis=0)
    grad_b_key = jnp.sum(grad_k_lin.astype(jnp.float32), axis=0)
    grad_b_value = jnp.sum(grad_v_lin.astype(jnp.float32), axis=0)
    grad_normed = lax.psum(
        (
            dot_right(grad_q_lin, w_query)
            + dot_right(grad_k_lin, w_key)
            + dot_right(grad_v_lin, w_value)
        ).astype(jnp.bfloat16),
        "tensor",
    ).astype(jnp.float32)
    grad_gain_attn = jnp.sum(grad_normed * stream * inverse_one, axis=0)
    scaled_one = grad_normed * gain_one
    grad_stream = (
        grad_resid
        + inverse_one * scaled_one
        - stream * inverse_one**3 * jnp.mean(scaled_one * stream, axis=-1, keepdims=True)
    )
    (
        statistics,
        grad_gain_attn,
        grad_w_query,
        grad_b_query,
        grad_w_key,
        grad_b_key,
        grad_w_value,
        grad_b_value,
        grad_w_out,
        grad_gain_mlp,
        grad_w_gate,
        grad_w_up,
        grad_w_down,
    ) = lax.psum(
        (
            statistics,
            grad_gain_attn,
            grad_w_query,
            grad_b_query,
            grad_w_key,
            grad_b_key,
            grad_w_value,
            grad_b_value,
            grad_w_out,
            grad_gain_mlp,
            grad_w_gate,
            grad_w_up,
            grad_w_down,
        ),
        "dp",
    )
    sent_back = (
        lax.all_to_all(
            result.astype(jnp.bfloat16)[None], "dp", split_axis=1, concat_axis=0, tiled=True
        ),
        lax.all_to_all(
            grad_stream.astype(jnp.bfloat16)[None], "dp", split_axis=1, concat_axis=0, tiled=True
        ),
    )
    layer_out = sent_back[0][restore]
    grad_tokens = sent_back[1][restore]
    count = jnp.sum(lengths).astype(jnp.float32) * width
    rms_values = jnp.sqrt(statistics / count)
    return (
        layer_out,
        grad_tokens,
        grad_gain_attn,
        grad_w_query,
        grad_b_query,
        grad_w_key,
        grad_b_key,
        grad_w_value,
        grad_b_value,
        grad_w_out,
        grad_gain_mlp,
        grad_w_gate,
        grad_w_up,
        grad_w_down,
        rms_values,
    )


def solution(mesh):
    in_specs = (
        P(None, "dp", None),
        P(None, "dp", None),
        P(),
        P(),
        P(),
        P(None, "tensor"),
        P("tensor"),
        P(None, "tensor"),
        P("tensor"),
        P(None, "tensor"),
        P("tensor"),
        P("tensor", None),
        P(),
        P(None, "tensor"),
        P(None, "tensor"),
        P("tensor", None),
    )
    out_specs = (
        P(None, "dp", None),
        P(None, "dp", None),
        P(),
        P(None, "tensor"),
        P("tensor"),
        P(None, "tensor"),
        P("tensor"),
        P(None, "tensor"),
        P("tensor"),
        P("tensor", None),
        P(),
        P(None, "tensor"),
        P(None, "tensor"),
        P("tensor", None),
        P(),
    )
    return jax.shard_map(
        on_device, mesh=mesh, in_specs=in_specs, out_specs=out_specs, check_vma=False
    )
```

profile of v0, /device:TPU:0, one launch (start us, length us, event | category | flops | bytes accessed | tf_op | source)
XLA Modules:
  0.0 1022.6 jit_solution(5831000406995036942)
XLA Ops:
  8.4 1.6 gather_fusion
  10.0 10.1 all-to-all-start
  22.0 14.5 %all-to-all-done = bf16[64,8,896]{2,1,0:T(8,128)(2,1)S(1)} async-done(((bf16[64,8,896]{2,1,0:T(8,128)(2,1)}), bf16[64,8,896]{2,1,0:T(8,128)(2,1)S(1)}, u32[]{:S(2)}, u32[]{:S(2)}) %all-to-all-start) | async-done | bytes 917536 | tf_op jit(solution)/shard_map/all_to_all | solution.py:77
  37.7 0.8 convolution_add_fusion.1
  38.7 1.3 fusion.6
  40.0 1.5 fusion.4
  42.1 0.8 copy-done.2
  42.9 2.3 fusion.36
  45.2 0.7 copy-done.8
  46.0 2.0 fusion.103
  48.0 1.6 gather_fusion.2
  49.6 5.5 all-to-all-start.2
  55.3 65.8 %all-reduce.8.cloned.1.call-done = f32[512,896]{1,0:T(8,128)} async-done(((f32[512,896]{1,0:T(8,128)}), f32[512,896]{1,0:T(8,128)}) %all-reduce.8.cloned.1.call-update) | async-done | bytes 1835024 | tf_op jit(solution)/shard_map/psum | solution.py:122
  121.1 1.8 multiply_reduce_fusion.3
  124.5 7.2 fusion.104
  131.7 4.5 fusion.105
  136.2 10.4 %multiply_convert_fusion = (bf16[512,2432]{1,0:T(8,128)(2,1)}, bf16[512,2432]{1,0:T(8,128)(2,1)}, bf16[512,2432]{1,0:T(8,128)(2,1)S(1)}) fusion(f32[512,2432]{1,0:T(8,128)} %fusion.104, f32[512,2432]{1,0:T(8,128)} %fusion.105, bf16[2432,896]{1,0:T(8,128)(2,1)} %param.31, bf16[64,8,896]{2,1,0:T(8,128)(2,1)} %all-to-all-done.2, ...), kind=kOutput, calls=%fused_computation.15 | convolution fusion | flops 2251423744 | bytes 22708736 | tf_op jit(solution)/shard_map/dot_general | solution.py:52
  146.6 1.5 copy-done.61
  148.0 6.0 convolution_convert_fusion
  154.1 6.0 fusion.106
  160.1 6.4 convolution_add_fusion
  167.7 8.2 fusion.108
  176.0 6.1 fusion.109
  182.1 7.5 fusion.65
  189.6 9.3 all-reduce.10.cloned.1.call-done
  198.9 67.2 %all-reduce.12.cloned.1.call-done = f32[512,896]{1,0:T(8,128)} async-done(((f32[512,896]{1,0:T(8,128)}), f32[512,896]{1,0:T(8,128)}) %all-reduce.12.cloned.1.call-update) | async-done | bytes 1835024 | tf_op jit(solution)/shard_map/psum | solution.py:152
  266.2 5.5 select_reduce_fusion
  271.8 2.5 fusion.35
  275.2 2.4 fusion
  277.6 2.4 fusion.7
  280.0 0.7 convolution_bitcast_fusion
  280.8 1.2 convolution_bitcast_fusion.1
  282.1 2.3 convert_reduce_fusion.1
  284.7 0.8 copy-done.15
  287.0 1.4 add_convert_fusion
  288.7 1.1 fusion.61
  289.8 1.1 fusion.63
  291.0 1.9 fusion.59
  292.9 1.8 fusion.56
  294.7 3.8 copy.64
  299.1 8.1 reduce.8
  307.2 2.9 reshape.436
  310.1 8.4 all-to-all-start.1
  318.5 22.4 %all-reduce.14.cloned.1.call-done = bf16[512,896]{1,0:T(8,128)(2,1)} async-done(((bf16[512,896]{1,0:T(8,128)(2,1)}), bf16[512,896]{1,0:T(8,128)(2,1)}) %all-reduce.14.cloned.1.call-update) | async-done | bytes 917520 | tf_op jit(solution)/shard_map/psum | solution.py:195
  340.9 2.0 fusion.29
  343.0 1.7 fusion.55
  344.7 1.4 copy.63
  346.1 6.2 reduce.9
  352.4 1.3 reshape.438
  353.7 8.3 all-to-all-start.3
  362.7 2.0 sort.17
  365.6 2.1 pad_maximum_fusion.3
  367.6 5.4 reshape.437
  373.0 1.0 copy.62
  374.1 2.8 gather_fusion.1
  376.8 280.9 %all-reduce = (f32[896]{0:T(1024)}, f32[448]{0:T(512)}, f32[64]{0:T(128)}, f32[64]{0:T(128)}, f32[896]{0:T(1024)}, /*index=5*/f32[3]{0:T(128)S(1)}) all-reduce(f32[896]{0:T(1024)S(1)} %get-tuple-element.20, f32[448]{0:T(512)S(1)} %reduce_sum.145, f32[64]{0:T(128)S(1)} %convert_reduce_fusion.2, ...), channel_id=1, replica_groups=mesh['dp'=64,'tensor'=2] {'dp'}, use_global_device_ids=true, to_apply=%region_13.14 | all-reduce | flops 2371 | bytes 18968 | tf_op jit(solution)/shard_map/psum | solution.py:224
  659.1 1.6 gather_fusion.3
  660.7 331.3 %all-reduce.16.cloned.1.call-done = (f32[896,448]{0,1:T(8,128)}, f32[896,64]{0,1:T(8,128)}, f32[896,64]{0,1:T(8,128)}, f32[448,896]{1,0:T(8,128)}, f32[896,2432]...) async-done(((f32[896,448]{0,1:T(8,128)}, f32[896,64]{0,1:T(8,128)}, f32[896,64]{0,1:T(8,128)}, f32[448,896]{1,0:T(8,128)}, f32[896,2432]{1,0:T(8,128)}, ...) | async-done | bytes 29818896 | tf_op jit(solution)/shard_map/psum | solution.py:224
  992.0 2.8 copy.76
  996.2 1.2 copy.79
  997.4 8.6 copy.80
  1006.0 4.4 copy.81
  1010.4 1.6 slice-done.3
  1012.1 3.5 copy.82
  (199 shorter events, 15.1 us)
Async XLA Ops:
  7.2 12.9 %copy-start.56 = (bf16[64]{0:T(256)(128)(2,1)S(1)}, bf16[64]{0:T(256)(128)(2,1)}, u32[]{:S(2)}) copy-start(bf16[64]{0:T(256)(128)(2,1)} %param.26) | copy-start | bytes 388
  7.2 12.9 %copy-start.53 = (bf16[896]{0:T(1024)(128)(2,1)S(1)}, bf16[896]{0:T(1024)(128)(2,1)}, u32[]{:S(2)}) copy-start(bf16[896]{0:T(1024)(128)(2,1)} %param.20) | copy-start | bytes 5380
  7.2 13.0 %copy-start.55 = (bf16[448]{0:T(512)(128)(2,1)S(1)}, bf16[448]{0:T(512)(128)(2,1)}, u32[]{:S(2)}) copy-start(bf16[448]{0:T(512)(128)(2,1)} %param.22) | copy-start | bytes 2692
  7.2 13.0 %copy-start.57 = (bf16[64]{0:T(256)(128)(2,1)S(1)}, bf16[64]{0:T(256)(128)(2,1)}, u32[]{:S(2)}) copy-start(bf16[64]{0:T(256)(128)(2,1)} %param.24) | copy-start | bytes 388
  7.2 13.0 %copy-start.58 = (s32[64]{0:T(128)S(1)}, s32[64]{0:T(128)}, u32[]{:S(2)}) copy-start(s32[64]{0:T(128)} %param.18) | copy-start | bytes 772
  8.4 28.5 %copy-start.26 = (bf16[896,64]{0,1:T(8,128)(2,1)S(1)}, bf16[896,64]{0,1:T(8,128)(2,1)}, u32[]{:S(2)}) copy-start(bf16[896,64]{0,1:T(8,128)(2,1)} %param.23) | copy-start | bytes 344068
  10.0 27.7 %copy-start.14 = (bf16[896,448]{0,1:T(8,128)(2,1)S(1)}, bf16[896,448]{0,1:T(8,128)(2,1)}, u32[]{:S(2)}) copy-start(bf16[896,448]{0,1:T(8,128)(2,1)} %param.21) | copy-start | bytes 2408452
  10.0 26.5 %all-to-all-start = ((bf16[64,8,896]{2,1,0:T(8,128)(2,1)}), bf16[64,8,896]{2,1,0:T(8,128)(2,1)S(1)}, u32[]{:S(2)}, u32[]{:S(2)}) async-start(bf16[64,8,896]{2,1,0:T(8,128)(2,1)} %gather_fusion), calls=%async_computation | async-start | bytes 1835008 | tf_op jit(solution)/shard_map/all_to_all | solution.py:77
  20.1 101.1 %all-reduce.8.cloned.1.call-start = ((), (), s32[]{:S(2)}) async-start(), calls=%async_computation.4 | async-start | bytes 3670016 | tf_op jit(solution)/shard_map/psum | solution.py:122
  20.2 21.4 %copy-start.38 = (f32[896]{0:T(1024)}, f32[896]{0:T(1024)S(1)}, u32[]{:S(2)}) copy-start(f32[896]{0:T(1024)S(1)} %convert_element_type.242) | copy-start | bytes 10756
  20.8 17.7 %copy-start.48 = (f32[32]{0:T(128)}, f32[32]{0:T(128)S(1)}, u32[]{:S(2)}) copy-start(f32[32]{0:T(128)S(1)} %multiply_power_fusion) | copy-start | bytes 388
  21.5 114.7 %copy-start.50 = (pred[512]{0:T(512)(128)(4,1)}, pred[512]{0:T(512)(128)(4,1)S(1)}, u32[]{:S(2)}) copy-start(pred[512]{0:T(512)(128)(4,1)S(1)} %iota_compare_fusion.1) | copy-start | bytes 1540
  21.5 17.0 %copy-start.42 = (f32[512]{0:T(512)}, f32[512]{0:T(512)S(1)}, u32[]{:S(2)}) copy-start(f32[512]{0:T(512)S(1)} %iota_convert_fusion) | copy-start | bytes 6148
  21.8 16.7 %copy-start.16 = (f32[512,32]{0,1:T(8,128)}, f32[512,32]{0,1:T(8,128)S(1)}, u32[]{:S(2)}) copy-start(f32[512,32]{0,1:T(8,128)S(1)} %get-tuple-element.58) | copy-start | bytes 196612
  36.9 4.7 copy-start.44
  37.7 2.3 copy-start.22
  37.7 2.3 copy-start.24
  40.0 2.9 copy-start.2
  40.0 2.9 copy-start.34
  41.6 3.6 copy-start.36
  42.9 3.1 copy-start.6
  45.2 2.7 copy-start.11
  47.9 7.4 copy-start.54
  49.6 86.6 %all-to-all-start.2 = ((bf16[64,8,896]{2,1,0:T(8,128)(2,1)}), bf16[64,8,896]{2,1,0:T(8,128)(2,1)}, u32[]{:S(2)}, u32[]{:S(2)}) async-start(bf16[64,8,896]{2,1,0:T(8,128)(2,1)} %gather_fusion.2), calls=%async_computation.2 | async-start | bytes 1835008 | tf_op jit(solution)/shard_map/all_to_all | solution.py:78
  55.0 143.9 %all-reduce.10.cloned.1.call-start = ((), (), s32[]{:S(2)}) async-start(), calls=%async_computation.5 | async-start | bytes 1835008 | tf_op jit(solution)/shard_map/psum | solution.py:131
  55.3 69.1 %copy-start.32 = (f32[896]{0:T(1024)}, f32[896]{0:T(1024)S(1)}, u32[]{:S(2)}) copy-start(f32[896]{0:T(1024)S(1)} %convert_element_type.255) | copy-start | bytes 10756
  123.0 143.2 %copy-start.3 = (f32[512,896]{1,0:T(8,128)}, f32[512,896]{1,0:T(8,128)S(1)}, u32[]{:S(2)}) copy-start(f32[512,896]{1,0:T(8,128)S(1)} %get-tuple-element.40) | copy-start | bytes 5505028
  124.2 7.5 slice-start.5
  124.4 7.2 copy-start.12
  124.5 7.2 slice-start.6
  154.1 112.1 %all-reduce.12.cloned.1.call-start = ((), (), s32[]{:S(2)}) async-start(), calls=%async_computation.6 | async-start | bytes 3670016 | tf_op jit(solution)/shard_map/psum | solution.py:152
  154.1 6.0 copy-start.63
  166.5 174.5 %all-reduce.14.cloned.1.call-start = ((), (), s32[]{:S(2)}) async-start(), calls=%async_computation.7 | async-start | bytes 1835008 | tf_op jit(solution)/shard_map/psum | solution.py:195
  167.7 8.3 copy-start.13
  167.7 8.3 copy-start.64
  175.9 6.1 copy-start.51
  175.9 6.1 copy-start.62
  266.1 5.6 copy-start.5
  266.1 5.6 copy-start.33
  266.1 5.6 copy-start.41
  266.1 5.6 copy-start.47
  266.1 5.6 copy-start.52
  266.2 8.8 slice-start
  271.7 2.5 copy-start.7
  271.8 3.2 slice-start.1
  277.6 2.4 copy-start.23
  277.6 2.4 copy-start.25
  282.0 2.3 copy-start.17
  288.4 703.6 %all-reduce.16.cloned.1.call-start = ((), (), s32[]{:S(2)}) async-start(), calls=%async_computation.8 | async-start | bytes 59637760 | tf_op jit(solution)/shard_map/psum | solution.py:224
  289.8 3.0 copy-start.9
  307.2 11.3 %copy-start.45 = (f32[512]{0:T(512)S(1)}, f32[512]{0:T(512)}, u32[]{:S(2)}) copy-start(f32[512]{0:T(512)} %copy-done.44) | copy-start | bytes 6148
  310.1 43.6 %all-to-all-start.1 = ((bf16[64,2,3584]{2,1,0:T(2,128)(2,1)}), bf16[64,2,3584]{2,1,0:T(2,128)(2,1)}, u32[]{:S(2)}, u32[]{:S(2)}) async-start(bf16[64,2,3584]{2,1,0:T(2,128)(2,1)} %reshape.436), calls=%async_computation.1 | async-start | bytes 1835008 | tf_op jit(solution)/shard_map/all_to_all | solution.py:243
  352.4 9.6 copy-start.59
  352.4 10.3 %copy-start.60 = (s32[64]{0:T(128)S(1)}, s32[64]{0:T(128)}, u32[]{:S(2)}) copy-start(s32[64]{0:T(128)} %param.19) | copy-start | bytes 772
  353.7 304.6 %all-to-all-start.3 = ((bf16[64,2,3584]{2,1,0:T(2,128)(2,1)}), bf16[64,2,3584]{2,1,0:T(2,128)(2,1)S(1)}, u32[]{:S(2)}, u32[]{:S(2)}) async-start(bf16[64,2,3584]{2,1,0:T(2,128)(2,1)} %reshape.438), calls=%async_computation.3 | async-start | bytes 1835008 | tf_op jit(solution)/shard_map/all_to_all | solution.py:246
  373.0 3.8 copy-start.46
  992.0 2.8 copy-start.21
  992.0 3.5 copy-start.20
  992.0 4.2 copy-start.10
  997.4 8.6 copy-start.4
  997.4 13.0 %slice-start.2 = ((s8[8716288]{0:T(1024)(128)(4,1)}), s8[4194304]{0:T(1024)(128)(4,1)S(1)}, s32[]{:S(2)}) async-start(s8[8716288]{0:T(1024)(128)(4,1)} %bitcast.213), calls=%async_computation.11 | async-start | bytes 8388608
  997.4 14.6 %slice-start.3 = ((s8[8716288]{0:T(1024)(128)(4,1)}), s8[4194304]{0:T(1024)(128)(4,1)S(1)}, s32[]{:S(2)}) async-start(s8[8716288]{0:T(1024)(128)(4,1)} %bitcast.213), calls=%async_computation.12 | async-start | bytes 8388608
  1006.0 6.1 slice-start.4
  1012.1 3.5 copy-start.1
  (17 other events, 24.8 us)
Sparse Core Ops, SparseCore 0:
  48.1 73.0 all-reduce.7
  154.2 44.6 all-reduce.9
  201.4 64.7 all-reduce.11
  288.6 52.3 all-reduce.13
  345.0 646.9 all-reduce.15
where the time goes:
time: 1030 us; the launch traced here: 1020 us
  waiting for transfers between devices  511 us (50%)
  blocking collectives  281 us (27%)
  matrix products  85.3 us (8%)
  local copies, waits for them, and re-layouts  54.4 us (5%)
  other arithmetic  42 us (4%)
  starting transfers between devices  33.3 us (3%)
  between operations  16 us (2%)
    psum x1, waiting for transfers between devices, on_device(): lax.psum((statistics, grad_gain_attn, grad_w_query, grad_b_query, grad_w_...  331 us
    psum x1, blocking collectives, on_device(): lax.psum((statistics, grad_gain_attn, grad_w_query, grad_b_query, grad_w_...  281 us
    psum x1, waiting for transfers between devices, on_device(): lax.psum(dot_right(grad_gate, w_gate) + dot_right(grad_up, w_up), 'tensor')  67.2 us
    psum x1, waiting for transfers between devices, on_device(): lax.psum(jnp.dot(mixed, w_out, preferred_element_type=jnp.float32), 'tens...  65.8 us
    unnamed x158, local copies, waits for them, and re-layouts  40.9 us
    dot_general x7, matrix products, dot_left(): lax.dot_general(matrix, other, (((0,), (0,)), ((), ())), preferred_elemen...  27.9 us
    dot_general x7, matrix products, dot_right(): lax.dot_general(matrix, other, (((1,), (1,)), ((), ())), preferred_elemen...  25.9 us
    psum x1, waiting for transfers between devices, on_device(): lax.psum((dot_right(grad_q_lin, w_query) + dot_right(grad_k_lin, w_key) +...  22.4 us
  transfers between devices with their start and end apart: 9, of which 6 were waited for; matrix products, arithmetic and copies ran while one was open for 10% of the time, Pallas kernels for 0%

commit v1 on v0

--- a/solution.py
+++ b/solution.py
@@ -149,7 +149,9 @@
     grad_up = (grad_hidden * silu_gate).astype(jnp.bfloat16)
     grad_w_gate = dot_left(normed_two, grad_gate)
     grad_w_up = dot_left(normed_two, grad_up)
-    grad_normed_two = lax.psum(dot_right(grad_gate, w_gate) + dot_right(grad_up, w_up), "tensor")
+    own = dot_right(grad_gate, w_gate) + dot_right(grad_up, w_up)
+    terms = lax.all_gather(own, "tensor", axis=0, tiled=False)
+    grad_normed_two = terms.sum(axis=0)
     grad_gain_mlp = jnp.sum(grad_normed_two * residual * inverse_two, axis=0)
     scaled_two = grad_normed_two * gain_two
     grad_resid = (

time: 1030 us -> 1030 us (level)
    psum x1 -> x0, waiting for transfers between devices: 67.2 us -> none  [on_device(): lax.psum(dot_right(grad_gate, w_gate) + dot_right(grad_up, w_up), 'tensor')]
    psum x1, waiting for transfers between devices: 9.31 us -> 44.1 us  [on_device(): lax.psum(jnp.dot(hidden, w_down, preferred_element_type=jnp.float32).asty...]
    all_gather x0 -> x1, waiting for transfers between devices: none -> 22.6 us  [on_device(): terms = lax.all_gather(own, 'tensor', axis=0, tiled=False)]
    unnamed x158 -> x156, local copies, waits for them, and re-layouts: 40.9 us -> 39.4 us
where the time goes in v1:
time: 1030 us; the launch traced here: 1020 us
  waiting for transfers between devices  501 us (49%)
  blocking collectives  281 us (27%)
  matrix products  88.5 us (9%)
  local copies, waits for them, and re-layouts  52.9 us (5%)
  other arithmetic  45.7 us (4%)
  starting transfers between devices  33.3 us (3%)
  between operations  16 us (2%)
    psum x1, waiting for transfers between devices, on_device(): lax.psum((statistics, grad_gain_attn, grad_w_query, grad_b_query, grad_w_...  331 us
    psum x1, blocking collectives, on_device(): lax.psum((statistics, grad_gain_attn, grad_w_query, grad_b_query, grad_w_...  281 us
    psum x1, waiting for transfers between devices, on_device(): lax.psum(jnp.dot(mixed, w_out, preferred_element_type=jnp.float32), 'tens...  65.8 us
    psum x1, waiting for transfers between devices, on_device(): lax.psum(jnp.dot(hidden, w_down, preferred_element_type=jnp.float32).asty...  44.1 us
    unnamed x156, local copies, waits for them, and re-layouts  39.4 us
    dot_general x7, matrix products, dot_left(): lax.dot_general(matrix, other, (((0,), (0,)), ((), ())), preferred_elemen...  30 us
    dot_general x7, matrix products, dot_right(): lax.dot_general(matrix, other, (((1,), (1,)), ((), ())), preferred_elemen...  26.4 us
    all_gather x1, waiting for transfers between devices, on_device(): terms = lax.all_gather(own, 'tensor', axis=0, tiled=False)  22.6 us
  transfers between devices with their start and end apart: 9, of which 6 were waited for; matrix products, arithmetic and copies ran while one was open for 10% of the time, Pallas kernels for 0%

profile of v1, /device:TPU:0, one launch (start us, length us, event | category | flops | bytes accessed | tf_op | source)
XLA Modules:
  0.0 1018.3 jit_solution(13982820181397536826)
XLA Ops:
  8.4 1.6 gather_fusion
  10.0 10.1 all-to-all-start
  22.0 14.5 %all-to-all-done = bf16[64,8,896]{2,1,0:T(8,128)(2,1)S(1)} async-done(((bf16[64,8,896]{2,1,0:T(8,128)(2,1)}), bf16[64,8,896]{2,1,0:T(8,128)(2,1)S(1)}, u32[]{:S(2)}, u32[]{:S(2)}) %all-to-all-start) | async-done | bytes 917536 | tf_op jit(solution)/shard_map/all_to_all | solution.py:77
  37.7 0.8 convolution_add_fusion.1
  38.7 1.3 fusion.6
  40.0 1.5 fusion.4
  42.1 0.8 copy-done.2
  42.9 2.3 fusion.36
  45.2 0.7 copy-done.8
  46.0 2.0 fusion.103
  48.0 1.6 gather_fusion.2
  49.6 5.5 all-to-all-start.2
  55.3 65.8 %all-reduce.7.cloned.1.call-done = f32[512,896]{1,0:T(8,128)} async-done(((f32[512,896]{1,0:T(8,128)}), f32[512,896]{1,0:T(8,128)}) %all-reduce.7.cloned.1.call-update) | async-done | bytes 1835024 | tf_op jit(solution)/shard_map/psum | solution.py:122
  121.2 1.8 multiply_reduce_fusion.3
  124.4 7.2 fusion.104
  131.7 4.5 fusion.105
  136.1 10.0 multiply_convert_fusion
  146.2 6.9 fusion.106
  153.1 6.4 convolution_add_fusion
  160.6 8.3 fusion.108
  168.9 6.5 convolution_convert_fusion
  175.5 8.2 fusion.109
  183.8 7.5 fusion.65
  191.3 22.6 %all-gather.3.cloned.1.call-done = f32[1024,896]{1,0:T(8,128)} async-done(((f32[512,896]{1,0:T(8,128)}), f32[1024,896]{1,0:T(8,128)}) %all-gather.3.cloned.1.call-update) | async-done | bytes 3670032 | tf_op jit(solution)/shard_map/all_gather | solution.py:153
  213.9 3.8 reduce_sum.149
  217.7 44.1 %all-reduce.9.cloned.1.call-done = bf16[512,896]{1,0:T(8,128)(2,1)} async-done(((bf16[512,896]{1,0:T(8,128)(2,1)}), bf16[512,896]{1,0:T(8,128)(2,1)}) %all-reduce.9.cloned.1.call-update) | async-done | bytes 917520 | tf_op jit(solution)/shard_map/psum | solution.py:131
  261.9 5.5 select_reduce_fusion
  267.4 2.5 fusion.35
  270.9 2.4 fusion
  273.3 2.4 fusion.7
  275.7 0.7 convolution_bitcast_fusion
  276.5 1.2 convolution_bitcast_fusion.1
  277.8 2.3 convert_reduce_fusion.1
  280.4 0.8 copy-done.14
  282.7 1.4 add_convert_fusion
  284.4 1.1 fusion.61
  285.5 1.1 fusion.63
  286.7 1.9 fusion.59
  288.6 1.8 fusion.56
  290.4 3.8 copy.64
  294.8 8.1 reduce.8
  302.9 2.9 reshape.437
  305.8 8.4 all-to-all-start.1
  314.2 22.4 %all-reduce.11.cloned.1.call-done = bf16[512,896]{1,0:T(8,128)(2,1)} async-done(((bf16[512,896]{1,0:T(8,128)(2,1)}), bf16[512,896]{1,0:T(8,128)(2,1)}) %all-reduce.11.cloned.1.call-update) | async-done | bytes 917520 | tf_op jit(solution)/shard_map/psum | solution.py:197
  336.7 2.0 fusion.29
  338.7 1.7 fusion.55
  340.4 1.4 copy.63
  341.8 6.2 reduce.9
  348.1 1.3 reshape.439
  349.4 8.3 all-to-all-start.3
  358.4 2.0 sort.17
  361.3 2.0 pad_maximum_fusion.3
  363.3 5.4 reshape.438
  368.7 1.0 copy.62
  369.7 2.8 gather_fusion.1
  372.5 280.9 %all-reduce = (f32[896]{0:T(1024)}, f32[448]{0:T(512)}, f32[64]{0:T(128)}, f32[64]{0:T(128)}, f32[896]{0:T(1024)}, /*index=5*/f32[3]{0:T(128)S(1)}) all-reduce(f32[896]{0:T(1024)S(1)} %get-tuple-element.20, f32[448]{0:T(512)S(1)} %reduce_sum.155, f32[64]{0:T(128)S(1)} %convert_reduce_fusion.2, ...), channel_id=1, replica_groups=mesh['dp'=64,'tensor'=2] {'dp'}, use_global_device_ids=true, to_apply=%region_13.14 | all-reduce | flops 2371 | bytes 18968 | tf_op jit(solution)/shard_map/psum | solution.py:226
  654.8 1.6 gather_fusion.3
  656.4 331.3 %all-reduce.13.cloned.1.call-done = (f32[896,448]{0,1:T(8,128)}, f32[896,64]{0,1:T(8,128)}, f32[896,64]{0,1:T(8,128)}, f32[448,896]{1,0:T(8,128)}, f32[896,2432]...) async-done(((f32[896,448]{0,1:T(8,128)}, f32[896,64]{0,1:T(8,128)}, f32[896,64]{0,1:T(8,128)}, f32[448,896]{1,0:T(8,128)}, f32[896,2432]{1,0:T(8,128)}, ...) | async-done | bytes 29818896 | tf_op jit(solution)/shard_map/psum | solution.py:226
  987.7 2.8 copy.75
  991.9 1.2 copy.78
  993.1 8.6 copy.79
  1001.7 4.4 copy.80
  1006.1 1.6 slice-done.3
  1007.8 3.5 copy.81
  (198 shorter events, 15.1 us)
Async XLA Ops:
  7.2 12.9 %copy-start.55 = (bf16[64]{0:T(256)(128)(2,1)S(1)}, bf16[64]{0:T(256)(128)(2,1)}, u32[]{:S(2)}) copy-start(bf16[64]{0:T(256)(128)(2,1)} %param.26) | copy-start | bytes 388
  7.2 12.9 %copy-start.52 = (bf16[896]{0:T(1024)(128)(2,1)S(1)}, bf16[896]{0:T(1024)(128)(2,1)}, u32[]{:S(2)}) copy-start(bf16[896]{0:T(1024)(128)(2,1)} %param.20) | copy-start | bytes 5380
  7.2 13.0 %copy-start.54 = (bf16[448]{0:T(512)(128)(2,1)S(1)}, bf16[448]{0:T(512)(128)(2,1)}, u32[]{:S(2)}) copy-start(bf16[448]{0:T(512)(128)(2,1)} %param.22) | copy-start | bytes 2692
  7.2 13.0 %copy-start.56 = (bf16[64]{0:T(256)(128)(2,1)S(1)}, bf16[64]{0:T(256)(128)(2,1)}, u32[]{:S(2)}) copy-start(bf16[64]{0:T(256)(128)(2,1)} %param.24) | copy-start | bytes 388
  7.2 13.0 %copy-start.57 = (s32[64]{0:T(128)S(1)}, s32[64]{0:T(128)}, u32[]{:S(2)}) copy-start(s32[64]{0:T(128)} %param.18) | copy-start | bytes 772
  8.4 28.5 %copy-start.25 = (bf16[896,64]{0,1:T(8,128)(2,1)S(1)}, bf16[896,64]{0,1:T(8,128)(2,1)}, u32[]{:S(2)}) copy-start(bf16[896,64]{0,1:T(8,128)(2,1)} %param.23) | copy-start | bytes 344068
  10.0 27.7 %copy-start.13 = (bf16[896,448]{0,1:T(8,128)(2,1)S(1)}, bf16[896,448]{0,1:T(8,128)(2,1)}, u32[]{:S(2)}) copy-start(bf16[896,448]{0,1:T(8,128)(2,1)} %param.21) | copy-start | bytes 2408452
  10.0 26.5 %all-to-all-start = ((bf16[64,8,896]{2,1,0:T(8,128)(2,1)}), bf16[64,8,896]{2,1,0:T(8,128)(2,1)S(1)}, u32[]{:S(2)}, u32[]{:S(2)}) async-start(bf16[64,8,896]{2,1,0:T(8,128)(2,1)} %gather_fusion), calls=%async_computation | async-start | bytes 1835008 | tf_op jit(solution)/shard_map/all_to_all | solution.py:77
  20.1 101.1 %all-reduce.7.cloned.1.call-start = ((), (), s32[]{:S(2)}) async-start(), calls=%async_computation.4 | async-start | bytes 3670016 | tf_op jit(solution)/shard_map/psum | solution.py:122
  20.2 21.4 %copy-start.37 = (f32[896]{0:T(1024)}, f32[896]{0:T(1024)S(1)}, u32[]{:S(2)}) copy-start(f32[896]{0:T(1024)S(1)} %convert_element_type.242) | copy-start | bytes 10756
  20.8 17.7 %copy-start.47 = (f32[32]{0:T(128)}, f32[32]{0:T(128)S(1)}, u32[]{:S(2)}) copy-start(f32[32]{0:T(128)S(1)} %multiply_power_fusion) | copy-start | bytes 388
  21.5 114.7 %copy-start.49 = (pred[512]{0:T(512)(128)(4,1)}, pred[512]{0:T(512)(128)(4,1)S(1)}, u32[]{:S(2)}) copy-start(pred[512]{0:T(512)(128)(4,1)S(1)} %iota_compare_fusion.1) | copy-start | bytes 1540
  21.5 17.0 %copy-start.41 = (f32[512]{0:T(512)}, f32[512]{0:T(512)S(1)}, u32[]{:S(2)}) copy-start(f32[512]{0:T(512)S(1)} %iota_convert_fusion) | copy-start | bytes 6148
  21.8 16.7 %copy-start.15 = (f32[512,32]{0,1:T(8,128)}, f32[512,32]{0,1:T(8,128)S(1)}, u32[]{:S(2)}) copy-start(f32[512,32]{0,1:T(8,128)S(1)} %get-tuple-element.58) | copy-start | bytes 196612
  36.9 4.7 copy-start.43
  37.7 2.3 copy-start.21
  37.7 2.3 copy-start.23
  40.0 2.9 copy-start.2
  40.0 2.9 copy-start.33
  41.6 3.6 copy-start.35
  42.9 3.1 copy-start.6
  45.2 2.7 copy-start.11
  47.9 7.4 copy-start.53
  49.6 86.6 %all-to-all-start.2 = ((bf16[64,8,896]{2,1,0:T(8,128)(2,1)}), bf16[64,8,896]{2,1,0:T(8,128)(2,1)}, u32[]{:S(2)}, u32[]{:S(2)}) async-start(bf16[64,8,896]{2,1,0:T(8,128)(2,1)} %gather_fusion.2), calls=%async_computation.2 | async-start | bytes 1835008 | tf_op jit(solution)/shard_map/all_to_all | solution.py:78
  55.0 158.9 %all-gather.3.cloned.1.call-start = ((), (), s32[]{:S(2)}) async-start(), calls=%async_computation.7 | async-start | bytes 5505024 | tf_op jit(solution)/shard_map/all_gather | solution.py:153
  55.3 69.1 %copy-start.31 = (f32[896]{0:T(1024)}, f32[896]{0:T(1024)S(1)}, u32[]{:S(2)}) copy-start(f32[896]{0:T(1024)S(1)} %convert_element_type.255) | copy-start | bytes 10756
  123.0 138.9 %copy-start.3 = (f32[512,896]{1,0:T(8,128)}, f32[512,896]{1,0:T(8,128)S(1)}, u32[]{:S(2)}) copy-start(f32[512,896]{1,0:T(8,128)S(1)} %get-tuple-element.40) | copy-start | bytes 5505028
  124.2 7.5 slice-start.5
  124.4 7.2 copy-start.12
  124.4 7.2 slice-start.6
  146.1 6.9 copy-start.63
  146.1 6.9 copy-start.62
  159.4 102.4 %all-reduce.9.cloned.1.call-start = ((), (), s32[]{:S(2)}) async-start(), calls=%async_computation.5 | async-start | bytes 1835008 | tf_op jit(solution)/shard_map/psum | solution.py:131
  160.6 8.3 copy-start.60
  175.5 161.2 %all-reduce.11.cloned.1.call-start = ((), (), s32[]{:S(2)}) async-start(), calls=%async_computation.6 | async-start | bytes 1835008 | tf_op jit(solution)/shard_map/psum | solution.py:197
  175.5 8.2 copy-start.50
  175.5 8.2 copy-start.61
  261.8 5.6 copy-start.4
  261.8 5.6 copy-start.32
  261.8 5.6 copy-start.40
  261.8 5.6 copy-start.46
  261.9 5.6 copy-start.51
  261.9 8.8 slice-start
  267.4 2.5 copy-start.7
  267.4 3.2 slice-start.1
  273.3 2.4 copy-start.22
  273.3 2.4 copy-start.24
  277.7 2.3 copy-start.16
  284.1 703.6 %all-reduce.13.cloned.1.call-start = ((), (), s32[]{:S(2)}) async-start(), calls=%async_computation.8 | async-start | bytes 59637760 | tf_op jit(solution)/shard_map/psum | solution.py:226
  285.5 3.0 copy-start.9
  302.9 11.3 %copy-start.44 = (f32[512]{0:T(512)S(1)}, f32[512]{0:T(512)}, u32[]{:S(2)}) copy-start(f32[512]{0:T(512)} %copy-done.43) | copy-start | bytes 6148
  305.8 43.6 %all-to-all-start.1 = ((bf16[64,2,3584]{2,1,0:T(2,128)(2,1)}), bf16[64,2,3584]{2,1,0:T(2,128)(2,1)}, u32[]{:S(2)}, u32[]{:S(2)}) async-start(bf16[64,2,3584]{2,1,0:T(2,128)(2,1)} %reshape.437), calls=%async_computation.1 | async-start | bytes 1835008 | tf_op jit(solution)/shard_map/all_to_all | solution.py:245
  348.1 9.6 copy-start.58
  348.1 10.3 %copy-start.59 = (s32[64]{0:T(128)S(1)}, s32[64]{0:T(128)}, u32[]{:S(2)}) copy-start(s32[64]{0:T(128)} %param.19) | copy-start | bytes 772
  349.4 304.6 %all-to-all-start.3 = ((bf16[64,2,3584]{2,1,0:T(2,128)(2,1)}), bf16[64,2,3584]{2,1,0:T(2,128)(2,1)S(1)}, u32[]{:S(2)}, u32[]{:S(2)}) async-start(bf16[64,2,3584]{2,1,0:T(2,128)(2,1)} %reshape.439), calls=%async_computation.3 | async-start | bytes 1835008 | tf_op jit(solution)/shard_map/all_to_all | solution.py:248
  368.7 3.8 copy-start.45
  987.7 2.8 copy-start.20
  987.7 3.5 copy-start.19
  987.7 4.2 copy-start.10
  993.1 8.6 copy-start.5
  993.1 13.0 %slice-start.2 = ((s8[8716288]{0:T(1024)(128)(4,1)}), s8[4194304]{0:T(1024)(128)(4,1)S(1)}, s32[]{:S(2)}) async-start(s8[8716288]{0:T(1024)(128)(4,1)} %bitcast.214), calls=%async_computation.11 | async-start | bytes 8388608
  993.1 14.6 %slice-start.3 = ((s8[8716288]{0:T(1024)(128)(4,1)}), s8[4194304]{0:T(1024)(128)(4,1)S(1)}, s32[]{:S(2)}) async-start(s8[8716288]{0:T(1024)(128)(4,1)} %bitcast.214), calls=%async_computation.12 | async-start | bytes 8388608
  1001.7 6.1 slice-start.4
  1007.8 3.5 copy-start.1
  (16 other events, 23.3 us)
Sparse Core Ops, SparseCore 0:
  48.1 73.0 all-reduce.6
  159.6 54.3 all-gather.2
  217.1 44.6 all-reduce.8
  284.2 52.3 all-reduce.10
  341.1 646.6 all-reduce.12
